TPU v7x, 512 devices: a whole 4x4x16 slice. The times are simulated.
512 devices in a mesh: energy: 32 (over x, z_lo), momentum: 16 (over z_hi, y, core).
Axes of the slice: x: 4, y: 4, z: 16 (z_hi: 2, z_lo: 8; z = z_hi * 8 + z_lo), core: 2. Of those that a mesh axis runs over, the one named last changes fastest.
Arguments:
- green_tiles: bfloat16 [16, 64, 4, 2, 128, 128], P('momentum', 'energy'), may hold values from -6 to 6
- dham_blocks: bfloat16 [3, 4, 2, 128, 128], replicated, may hold values from -0.375 to 0.375
- phonon_weight: float32 [6, 3, 2], replicated, may hold values from 0.1 to 0.5
- phonon_modes: int32 [6, 2], replicated, may hold values from -1 to 2, as said below
- tile_pattern: int32 [4, 2], replicated, may hold values from 0 to 3, as said below
Outputs:
- self_energy: bfloat16 [16, 64, 4, 2, 128, 128], P('momentum', 'energy')
Inputs may be any that keep to these rules, and one draw needn't show every extreme that they name: `phonon_modes`: column 0 is a momentum offset and each of -1, 0, 1 is used by some mode; column 1 is an energy offset and each of 1 to 2 is used by some mode. `tile_pattern`: every block number appears in each column.
All inputs are finite; a program needn't handle non-finite values.
Results may differ from a plain program's by a relative error of at most 0.0062.
Values may be sent and summed in bfloat16 or wider, within the bound.
A program may use at most 64 MiB of HBM per device.

v0:
```python
import jax
import jax.numpy as jnp
from jax import lax
from jax.sharding import PartitionSpec as P

OFFSETS = (-1, 0, 1)


def with_halo(block, sides, width):
    for axis, dim in sides:
        count = lax.axis_size(axis)
        forward = [(i, i + 1) for i in range(count - 1)]
        backward = [(target, source) for source, target in forward]
        low = lax.ppermute(
            lax.slice_in_dim(block, block.shape[dim] - width, None, axis=dim), axis, forward
        )
        high = lax.ppermute(lax.slice_in_dim(block, 0, width, axis=dim), axis, backward)
        block = jnp.concatenate([low, block, high], axis=dim)
    return block


def from_behind(block, axis, distance):
    devices = range(lax.axis_size(axis))
    route = [((i - distance) % len(devices), i) for i in devices]
    return lax.ppermute(block, axis, route)


def stack_blocks(left_sel, right_sel):
    left_real = left_sel[:, :, 0]
    left_imag = left_sel[:, :, 1]
    upper_row = jnp.stack([left_real, -left_imag], axis=3)
    lower_row = jnp.stack([left_imag, left_real], axis=3)
    left_big = jnp.stack([upper_row, lower_row], axis=2)
    right_real = jnp.swapaxes(right_sel[:, :, 0], -1, -2)
    right_imag = jnp.swapaxes(right_sel[:, :, 1], -1, -2)
    first_col = jnp.stack([right_real, -right_imag], axis=3)
    second_col = jnp.stack([right_imag, right_real], axis=3)
    right_big = jnp.stack([first_col, second_col], axis=2)
    return (left_big, right_big)


def coupling(phonon_modes, phonon_weight, offset, energy_count):
    span = jnp.arange(-energy_count, energy_count + 1, dtype=jnp.int32)
    chosen = (phonon_modes[:, 0] == offset).astype(jnp.float32)
    below = (span[None, :] == -phonon_modes[:, 1:2]).astype(jnp.float32)
    above = (span[None, :] == phonon_modes[:, 1:2]).astype(jnp.float32)
    terms = chosen[:, None, None] * (
        phonon_weight[:, :, 0:1] * below[:, None, :] + phonon_weight[:, :, 1:2] * above[:, None, :]
    )
    return jnp.sum(terms, axis=0).astype(jnp.bfloat16)


def band_matrix(kern, energy_count):
    relative = (
        jnp.arange(3 * energy_count, dtype=jnp.int32)[None, :]
        - energy_count
        - jnp.arange(energy_count, dtype=jnp.int32)[:, None]
    )
    span = jnp.arange(-energy_count, energy_count + 1, dtype=jnp.int32)
    onehot = (relative[:, :, None] == span[None, None, :]).astype(jnp.float32)
    table = jnp.einsum(
        "dx,ejx->dej", kern.astype(jnp.float32), onehot, precision=lax.Precision.HIGHEST
    )
    return table.astype(jnp.bfloat16).reshape(3 * energy_count, 3 * energy_count)


def contribution(window, table, left_big, right_big):
    energy_count = window.shape[0] // 3
    flat = window.reshape(window.shape[0], -1)
    mixed = jnp.dot(table, flat, preferred_element_type=jnp.float32).astype(jnp.bfloat16)
    mixed = mixed.reshape((3, energy_count) + window.shape[1:])
    product = jnp.einsum(
        "dtbicj,detcjk->detbik", left_big, mixed, preferred_element_type=jnp.float32
    ).astype(jnp.bfloat16)
    return jnp.einsum(
        "detcij,dtcjbk->etbik", product, right_big, preferred_element_type=jnp.float32
    )


def local(green_tiles, dham_blocks, phonon_weight, phonon_modes, tile_pattern):
    energy_count = green_tiles.shape[1]
    tile_count = green_tiles.shape[2]
    tile_size = green_tiles.shape[4]
    block_count = dham_blocks.shape[1]
    block_ids = jnp.arange(block_count, dtype=jnp.int32)[None, :]
    choose_left = (tile_pattern[:, 0:1] == block_ids).astype(jnp.bfloat16)
    choose_right = (tile_pattern[:, 1:2] == block_ids).astype(jnp.bfloat16)
    left_sel = jnp.einsum(
        "tb,dbcij->dtcij", choose_left, dham_blocks, preferred_element_type=jnp.float32
    ).astype(jnp.bfloat16)
    right_sel = jnp.einsum(
        "tb,dbcij->dtcij", choose_right, dham_blocks, preferred_element_type=jnp.float32
    ).astype(jnp.bfloat16)
    left_big, right_big = stack_blocks(left_sel, right_sel)
    tables = [
        band_matrix(coupling(phonon_modes, phonon_weight, offset, energy_count), energy_count)
        for offset in OFFSETS
    ]
    packed = green_tiles.reshape(1, energy_count * tile_count, 2, tile_size, tile_size)
    window_shape = (3 * energy_count, tile_count, 2, tile_size, tile_size)
    summed = jnp.zeros((energy_count, tile_count, 2, tile_size, tile_size), jnp.float32)
    own_window = with_halo(packed, (("energy", 0),), 1)
    for position, offset in enumerate(OFFSETS):
        arrived = own_window
        if offset != 0:
            arrived = from_behind(own_window, "momentum", offset)
        summed = summed + contribution(
            arrived.reshape(window_shape), tables[position], left_big, right_big
        )
    return summed.astype(jnp.bfloat16)[None]


def solution(mesh):
    placed = (P("momentum", "energy", None, None, None, None), P(), P(), P(), P())
    return jax.shard_map(
        local,
        mesh=mesh,
        in_specs=placed,
        out_specs=P("momentum", "energy", None, None, None, None),
        check_vma=False,
    )
```

profile of v0, /device:TPU:36, one launch (start us, length us, event | category | flops | bytes accessed | tf_op | source)
XLA Modules:
  0.0 148.8 jit_solution(3792087853784038771)
XLA Ops:
  0.0 3.9 %collective-permute-start = (bf16[1,8,2,128,128]{4,3,2,1,0:T(8,128)(2,1)}, bf16[1,8,2,128,128]{4,3,2,1,0:T(8,128)(2,1)S(1)}, u32[]{:S(2)}, u32[]{:S(2)}) collective-permute-start(bf16[1,8,2,128,128]{4,3,2,1,0:T(8,128)(2,1)} %bitcast.212), channel_id=1, source_target_pairs={{0,16},{16,32},{32,48},{48,64},{64,80},{80,96},{96,112},{112,128},... | collective-permute-start | bytes 1572872 | tf_op jit(solution)/shard_map/ppermute | solution.py:14
  4.0 2.0 %collective-permute-start.1 = (bf16[1,8,2,128,128]{4,3,2,1,0:T(8,128)(2,1)}, bf16[1,8,2,128,128]{4,3,2,1,0:T(8,128)(2,1)S(1)}, u32[]{:S(2)}, u32[]{:S(2)}) collective-permute-start(bf16[1,8,2,128,128]{4,3,2,1,0:T(8,128)(2,1)} %bitcast.213), channel_id=1, source_target_pairs={{16,0},{32,16},{48,32},{64,48},{80,64},{96,80},{112,96},{128,112},... | collective-permute-start | bytes 1572872 | tf_op jit(solution)/shard_map/ppermute | solution.py:17
  6.0 0.7 negate_bitcast_fusion
  6.7 0.7 fusion.91
  7.4 0.8 fusion.95
  8.4 0.8 slice_bitcast_fusion.5
  9.8 0.8 fusion.49
  11.3 15.4 %collective-permute-done = bf16[1,8,2,128,128]{4,3,2,1,0:T(8,128)(2,1)S(1)} collective-permute-done((bf16[1,8,2,128,128]{4,3,2,1,0:T(8,128)(2,1)}, bf16[1,8,2,128,128]{4,3,2,1,0:T(8,128)(2,1)S(1)}, u32[]{:S(2)}, u32[]{:S(2)}) %collective-permute-start) | collective-permute-done | bytes 524320 | tf_op jit(solution)/shard_map/ppermute | solution.py:14
  26.7 4.2 %collective-permute-done.1 = bf16[1,8,2,128,128]{4,3,2,1,0:T(8,128)(2,1)S(1)} collective-permute-done((bf16[1,8,2,128,128]{4,3,2,1,0:T(8,128)(2,1)}, bf16[1,8,2,128,128]{4,3,2,1,0:T(8,128)(2,1)S(1)}, u32[]{:S(2)}, u32[]{:S(2)}) %collective-permute-start.1) | collective-permute-done | bytes 524320 | tf_op jit(solution)/shard_map/ppermute | solution.py:17
  30.9 1.3 pad_maximum_fusion
  32.2 14.4 %collective-permute-start.2 = (bf16[3,8,2,128,128]{4,3,2,1,0:T(8,128)(2,1)}, bf16[3,8,2,128,128]{4,3,2,1,0:T(8,128)(2,1)}, u32[]{:S(2)}, u32[]{:S(2)}) collective-permute-start(bf16[3,8,2,128,128]{4,3,2,1,0:T(8,128)(2,1)} %pad_maximum_fusion), channel_id=1, source_target_pairs={{1,0},{2,1},{3,2},{4,3},{5,4},{6,5},{7,6},{8,7},{9,8},{10,9},{11,1... | collective-permute-start | bytes 4718600 | tf_op jit(solution)/shard_map/ppermute | solution.py:25
  46.6 0.8 maximum_bitcast_fusion.2
  47.5 2.1 %collective-permute-start.3 = (bf16[3,8,2,128,128]{4,3,2,1,0:T(8,128)(2,1)}, bf16[3,8,2,128,128]{4,3,2,1,0:T(8,128)(2,1)}, u32[]{:S(2)}, u32[]{:S(2)}) collective-permute-start(bf16[3,8,2,128,128]{4,3,2,1,0:T(8,128)(2,1)} %pad_maximum_fusion), channel_id=1, source_target_pairs={{15,0},{0,1},{1,2},{2,3},{3,4},{4,5},{5,6},{6,7},{7,8},{8,9},{9,10... | collective-permute-start | bytes 4718600 | tf_op jit(solution)/shard_map/ppermute | solution.py:25
  49.6 2.3 %maximum_bitcast_fusion = bf16[3,4,2,128,2,128,1]{3,1,5,0,4,2,6:T(4,128)(2,1)} fusion(bf16[3,4,1,128,2,128]{3,1,5,0,4,2:T(4,128)(2,1)S(1)} %get-tuple-element.13, bf16[3,4,1,128,2,128]{3,1,5,0,4,2:T(4,128)(2,1)S(1)} %get-tuple-element.12), kind=kLoop, calls=%fused_computation.9 | loop fusion | flops 786432 | bytes 3145728 | tf_op jit(solution)/shard_map/stack | solution.py:38
  51.9 0.8 fusion.50
  53.2 0.8 maximum_bitcast_fusion.4
  54.0 2.3 %maximum_bitcast_fusion.1 = bf16[3,4,2,128,2,128,1]{5,1,3,0,4,2,6:T(4,128)(2,1)} fusion(bf16[3,4,1,128,2,128]{5,1,3,0,4,2:T(4,128)(2,1)S(1)} %get-tuple-element.15, bf16[3,4,1,128,2,128]{5,1,3,0,4,2:T(4,128)(2,1)S(1)} %get-tuple-element.14), kind=kLoop, calls=%fused_computation.11 | loop fusion | flops 786432 | bytes 3145728 | tf_op jit(solution)/shard_map/stack | solution.py:33
  56.3 3.0 %reshape_reshape.10 = bf16[6,131072]{1,0:T(8,128)(2,1)S(1)} reshape(bf16[3,8,2,128,128]{4,3,2,1,0:T(8,128)(2,1)} %pad_maximum_fusion) | data formatting | bytes 3145728 | tf_op jit(solution)/shard_map/reshape;reshape | solution.py:69
  59.3 0.7 fusion.1
  60.0 1.4 copy.127
  61.4 54.1 %collective-permute-done.2 = bf16[3,8,2,128,128]{4,3,2,1,0:T(8,128)(2,1)} collective-permute-done((bf16[3,8,2,128,128]{4,3,2,1,0:T(8,128)(2,1)}, bf16[3,8,2,128,128]{4,3,2,1,0:T(8,128)(2,1)}, u32[]{:S(2)}, u32[]{:S(2)}) %collective-permute-start.2) | collective-permute-done | bytes 1572896 | tf_op jit(solution)/shard_map/ppermute | solution.py:25
  115.5 3.0 %reshape_reshape.9 = bf16[6,131072]{1,0:T(8,128)(2,1)S(1)} reshape(bf16[3,8,2,128,128]{4,3,2,1,0:T(8,128)(2,1)} %collective-permute-done.2) | data formatting | bytes 3145728 | tf_op jit(solution)/shard_map/reshape;reshape | solution.py:69
  118.5 0.7 fusion
  119.2 1.4 copy.126
  120.7 10.4 %collective-permute-done.3 = bf16[3,8,2,128,128]{4,3,2,1,0:T(8,128)(2,1)} collective-permute-done((bf16[3,8,2,128,128]{4,3,2,1,0:T(8,128)(2,1)}, bf16[3,8,2,128,128]{4,3,2,1,0:T(8,128)(2,1)}, u32[]{:S(2)}, u32[]{:S(2)}) %collective-permute-start.3) | collective-permute-done | bytes 1572896 | tf_op jit(solution)/shard_map/ppermute | solution.py:25
  131.0 3.0 %reshape_reshape.11 = bf16[6,131072]{1,0:T(8,128)(2,1)S(1)} reshape(bf16[3,8,2,128,128]{4,3,2,1,0:T(8,128)(2,1)} %collective-permute-done.3) | data formatting | bytes 3145728 | tf_op jit(solution)/shard_map/reshape;reshape | solution.py:69
  134.1 0.9 fusion.2
  135.0 1.4 copy.128
  136.4 4.6 %fusion.24 = f32[4,2,128,2,128]{4,2,3,1,0:T(8,128)} fusion(bf16[3,2,4,2,128,128,1]{5,4,3,2,1,0,6:T(8,128)(2,1)} %bitcast.210, bf16[3,4,2,128,2,128,1]{5,1,3,0,4,2,6:T(4,128)(2,1)} %maximum_bitcast_fusion.1, bf16[3,4,2,128,2,128,1]{3,1,5,0,4,2,6:T(4,128)(2,1)} %maximum_bitcast_fusion), kind=kOutput, calls=%fused_computation.23 | convolution fusion | flops 806092800 | bytes 5767168 | tf_op jit(solution)/shard_map/detcij,dtcjbk->etbik/dot_general | solution.py:75
  141.0 3.3 %fusion.44 = f32[4,2,128,2,128]{4,2,3,1,0:T(8,128)S(1)} fusion(f32[4,2,128,2,128]{4,2,3,1,0:T(8,128)} %fusion.24, bf16[3,2,4,2,128,128,1]{5,4,3,2,1,0,6:T(8,128)(2,1)S(1)} %bitcast.209, bf16[3,4,2,128,2,128,1]{5,1,3,0,4,2,6:T(4,128)(2,1)} %maximum_bitcast_fusion.1, bf16[3,4,2,128,2,128,1]{3,1,5,0,4,2,6:T(4,128)(2,1)} %maximum_bitcast_fusion), kind=kOutput, calls=%fused_computation.27 | convolution fusion | flops 806354944 | bytes 6815744 | tf_op jit(solution)/shard_map/detcij,dtcjbk->etbik/dot_general | solution.py:75
  144.3 3.5 %fusion.56 = bf16[1,2,4,2,128,128]{4,5,1,3,2,0:T(8,128)(2,1)S(1)} fusion(f32[4,2,128,2,128]{4,2,3,1,0:T(8,128)S(1)} %fusion.44, bf16[3,2,4,2,128,128,1]{5,4,3,2,1,0,6:T(8,128)(2,1)} %bitcast.211, bf16[3,4,2,128,2,128,1]{5,1,3,0,4,2,6:T(4,128)(2,1)} %maximum_bitcast_fusion.1, bf16[3,4,2,128,2,128,1]{3,1,5,0,4,2,6:T(4,128)(2,1)} %maximum_bitcast_fusion), kind=kOutput, calls=%fused_computation.31 | convolution fusion | flops 806617088 | bytes 6291456 | tf_op jit(solution)/shard_map/detcij,dtcjbk->etbik/dot_general | solution.py:75
  147.8 1.0 copy.77
  (28 shorter events, 2.1 us)
Async XLA Ops:
  0.0 9.8 %copy-start = (bf16[3,4,2,128,128]{4,3,2,1,0:T(8,128)(2,1)S(1)}, bf16[3,4,2,128,128]{4,3,2,1,0:T(8,128)(2,1)}, u32[]{:S(2)}) copy-start(bf16[3,4,2,128,128]{4,3,2,1,0:T(8,128)(2,1)} %param.6) | copy-start | bytes 2359300
  0.0 26.7 %collective-permute-start = (bf16[1,8,2,128,128]{4,3,2,1,0:T(8,128)(2,1)}, bf16[1,8,2,128,128]{4,3,2,1,0:T(8,128)(2,1)S(1)}, u32[]{:S(2)}, u32[]{:S(2)}) collective-permute-start(bf16[1,8,2,128,128]{4,3,2,1,0:T(8,128)(2,1)} %bitcast.212), channel_id=1, source_target_pairs={{0,16},{16,32},{32,48},{48,64},{64,80},{80,96},{96,112},{112,128},... | collective-permute-start | bytes 1572872 | tf_op jit(solution)/shard_map/ppermute | solution.py:14
  4.0 26.9 %collective-permute-start.1 = (bf16[1,8,2,128,128]{4,3,2,1,0:T(8,128)(2,1)}, bf16[1,8,2,128,128]{4,3,2,1,0:T(8,128)(2,1)S(1)}, u32[]{:S(2)}, u32[]{:S(2)}) collective-permute-start(bf16[1,8,2,128,128]{4,3,2,1,0:T(8,128)(2,1)} %bitcast.213), channel_id=1, source_target_pairs={{16,0},{32,16},{48,32},{64,48},{80,64},{96,80},{112,96},{128,112},... | collective-permute-start | bytes 1572872 | tf_op jit(solution)/shard_map/ppermute | solution.py:17
  10.6 20.3 %copy-start.2 = (bf16[1,2,4,2,128,128]{5,4,3,2,1,0:T(8,128)(2,1)S(1)}, bf16[1,2,4,2,128,128]{5,4,3,2,1,0:T(8,128)(2,1)}, u32[]{:S(2)}) copy-start(bf16[1,2,4,2,128,128]{5,4,3,2,1,0:T(8,128)(2,1)} %param.5) | copy-start | bytes 1572868
  32.2 83.3 %collective-permute-start.2 = (bf16[3,8,2,128,128]{4,3,2,1,0:T(8,128)(2,1)}, bf16[3,8,2,128,128]{4,3,2,1,0:T(8,128)(2,1)}, u32[]{:S(2)}, u32[]{:S(2)}) collective-permute-start(bf16[3,8,2,128,128]{4,3,2,1,0:T(8,128)(2,1)} %pad_maximum_fusion), channel_id=1, source_target_pairs={{1,0},{2,1},{3,2},{4,3},{5,4},{6,5},{7,6},{8,7},{9,8},{10,9},{11,1... | collective-permute-start | bytes 4718600 | tf_op jit(solution)/shard_map/ppermute | solution.py:25
  47.5 83.6 %collective-permute-start.3 = (bf16[3,8,2,128,128]{4,3,2,1,0:T(8,128)(2,1)}, bf16[3,8,2,128,128]{4,3,2,1,0:T(8,128)(2,1)}, u32[]{:S(2)}, u32[]{:S(2)}) collective-permute-start(bf16[3,8,2,128,128]{4,3,2,1,0:T(8,128)(2,1)} %pad_maximum_fusion), channel_id=1, source_target_pairs={{15,0},{0,1},{1,2},{2,3},{3,4},{4,5},{5,6},{6,7},{7,8},{8,9},{9,10... | collective-permute-start | bytes 4718600 | tf_op jit(solution)/shard_map/ppermute | solution.py:25
  136.4 4.6 %copy-start.1 = (bf16[1,6,1024,128]{3,2,1,0:T(8,128)(2,1)S(1)}, bf16[1,6,1024,128]{3,2,1,0:T(8,128)(2,1)}, u32[]{:S(2)}) copy-start(bf16[1,6,1024,128]{3,2,1,0:T(8,128)(2,1)} %copy.127) | copy-start | bytes 4718596
where the time goes:
time: 149 us
  waiting for transfers between devices  84 us (56%)
  starting transfers between devices  22.5 us (15%)
  local copies, waits for them, and re-layouts  16.8 us (11%)
  matrix products  15.9 us (11%)
  other arithmetic  9.47 us (6%)
    ppermute x2, waiting for transfers between devices, from_behind(): return lax.ppermute(block, axis, route)  64.5 us
    ppermute x2, starting transfers between devices, from_behind(): return lax.ppermute(block, axis, route)  16.5 us
    ppermute x1, waiting for transfers between devices, with_halo(): lax.ppermute(lax.slice_in_dim(block, block.shape[dim] - width, None, axis...  15.4 us
    dot_general x3, matrix products, contribution(): jnp.einsum('detcij,dtcjbk->etbik', product, right_big, preferred_element_...  11.4 us
    another operation x3, local copies, waits for them, and re-layouts, contribution(): flat = window.reshape(window.shape[0], -1)  9.15 us
    unnamed x13, local copies, waits for them, and re-layouts  4.51 us
    ppermute x1, waiting for transfers between devices, with_halo(): lax.ppermute(lax.slice_in_dim(block, 0, width, axis=dim), axis, backward)  4.16 us
    ppermute x1, starting transfers between devices, with_halo(): lax.ppermute(lax.slice_in_dim(block, block.shape[dim] - width, None, axis...  3.95 us
  transfers between devices with their start and end apart: 4, of which 4 were waited for; matrix products, arithmetic and copies ran while one was open for 15% of the time, Pallas kernels for 0%

commit v1 on v0

--- a/solution.py
+++ b/solution.py
@@ -101,12 +101,10 @@
     summed = jnp.zeros((energy_count, tile_count, 2, tile_size, tile_size), jnp.float32)
     own_window = with_halo(packed, (("energy", 0),), 1)
     for position, offset in enumerate(OFFSETS):
-        arrived = own_window
+        term = contribution(own_window.reshape(window_shape), tables[position], left_big, right_big)
         if offset != 0:
-            arrived = from_behind(own_window, "momentum", offset)
-        summed = summed + contribution(
-            arrived.reshape(window_shape), tables[position], left_big, right_big
-        )
+            term = from_behind(term.astype(jnp.bfloat16), "momentum", offset).astype(jnp.float32)
+        summed = summed + term
     return summed.astype(jnp.bfloat16)[None]
 
 

time: 149 us -> 105 us (0.70)
  the two profiles are of different devices: /device:TPU:36 before, /device:TPU:63 now
where the time goes in v1:
time: 105 us; the launch traced here: 104 us
  waiting for transfers between devices  52.9 us (50%)
  starting transfers between devices  16.7 us (16%)
  matrix products  16.2 us (15%)
  other arithmetic  9.45 us (9%)
  local copies, waits for them, and re-layouts  8.96 us (9%)
    ppermute x2, waiting for transfers between devices, from_behind(): return lax.ppermute(block, axis, route)  34.5 us
    ppermute x1, waiting for transfers between devices, with_halo(): lax.ppermute(lax.slice_in_dim(block, block.shape[dim] - width, None, axis...  18.3 us
    dot_general x3, matrix products, contribution(): jnp.einsum('detcij,dtcjbk->etbik', product, right_big, preferred_element_...  11.9 us
    ppermute x2, starting transfers between devices, from_behind(): return lax.ppermute(block, axis, route)  11.1 us
    ppermute x1, starting transfers between devices, with_halo(): lax.ppermute(lax.slice_in_dim(block, block.shape[dim] - width, None, axis...  3.55 us
    unnamed x13, local copies, waits for them, and re-layouts  3.48 us
    another operation x2, other arithmetic, stack_blocks(): left_big = jnp.stack([upper_row, lower_row], axis=2)  3.11 us
    another operation x2, other arithmetic, stack_blocks(): right_big = jnp.stack([first_col, second_col], axis=2)  3.11 us
  transfers between devices with their start and end apart: 4, of which 3 were waited for; matrix products, arithmetic and copies ran while one was open for 18% of the time, Pallas kernels for 0%

profile of v1, /device:TPU:63, one launch (start us, length us, event | category | flops | bytes accessed | tf_op | source)
XLA Modules:
  0.0 104.3 jit_solution(1151120887687312589)
XLA Ops:
  0.0 2.0 %collective-permute-start.1 = (bf16[1,8,2,128,128]{4,3,2,1,0:T(8,128)(2,1)}, bf16[1,8,2,128,128]{4,3,2,1,0:T(8,128)(2,1)S(1)}, u32[]{:S(2)}, u32[]{:S(2)}) collective-permute-start(bf16[1,8,2,128,128]{4,3,2,1,0:T(8,128)(2,1)} %bitcast.218), channel_id=1, source_target_pairs={{16,0},{32,16},{48,32},{64,48},{80,64},{96,80},{112,96},{128,112},... | collective-permute-start | bytes 1572872 | tf_op jit(solution)/shard_map/ppermute | solution.py:17
  2.1 3.5 %collective-permute-start = (bf16[1,8,2,128,128]{4,3,2,1,0:T(8,128)(2,1)}, bf16[1,8,2,128,128]{4,3,2,1,0:T(8,128)(2,1)S(1)}, u32[]{:S(2)}, u32[]{:S(2)}) collective-permute-start(bf16[1,8,2,128,128]{4,3,2,1,0:T(8,128)(2,1)} %bitcast.219), channel_id=1, source_target_pairs={{0,16},{16,32},{32,48},{48,64},{64,80},{80,96},{96,112},{112,128},... | collective-permute-start | bytes 1572872 | tf_op jit(solution)/shard_map/ppermute | solution.py:14
  5.6 0.7 negate_bitcast_fusion
  6.3 0.7 fusion.93
  7.0 0.8 slice_bitcast_fusion.5
  7.8 0.8 fusion.39
  8.7 0.3 slice_bitcast_fusion.3
  9.0 0.2 copy-done.2
  9.9 0.2 convolution_convert_fusion.5
  10.1 0.8 fusion.40
  10.9 0.3 slice_bitcast_fusion
  11.2 0.8 maximum_bitcast_fusion.2
  12.0 2.3 %maximum_bitcast_fusion = bf16[3,4,2,128,2,128,1]{3,1,5,0,4,2,6:T(4,128)(2,1)} fusion(bf16[3,4,1,128,2,128]{3,1,5,0,4,2:T(4,128)(2,1)S(1)} %get-tuple-element.13, bf16[3,4,1,128,2,128]{3,1,5,0,4,2:T(4,128)(2,1)S(1)} %get-tuple-element.12), kind=kLoop, calls=%fused_computation.9 | loop fusion | flops 786432 | bytes 3145728 | tf_op jit(solution)/shard_map/stack | solution.py:38
  14.5 0.8 maximum_bitcast_fusion.4
  15.3 2.3 %maximum_bitcast_fusion.1 = bf16[3,4,2,128,2,128,1]{5,1,3,0,4,2,6:T(4,128)(2,1)} fusion(bf16[3,4,1,128,2,128]{5,1,3,0,4,2:T(4,128)(2,1)S(1)} %get-tuple-element.15, bf16[3,4,1,128,2,128]{5,1,3,0,4,2:T(4,128)(2,1)S(1)} %get-tuple-element.14), kind=kLoop, calls=%fused_computation.11 | loop fusion | flops 786432 | bytes 3145728 | tf_op jit(solution)/shard_map/stack | solution.py:33
  17.6 18.3 %collective-permute-done = bf16[1,8,2,128,128]{4,3,2,1,0:T(8,128)(2,1)S(1)} collective-permute-done((bf16[1,8,2,128,128]{4,3,2,1,0:T(8,128)(2,1)}, bf16[1,8,2,128,128]{4,3,2,1,0:T(8,128)(2,1)S(1)}, u32[]{:S(2)}, u32[]{:S(2)}) %collective-permute-start) | collective-permute-done | bytes 524320 | tf_op jit(solution)/shard_map/ppermute | solution.py:14
  35.9 1.3 %pad_maximum_fusion = bf16[3,8,2,128,128]{4,3,2,1,0:T(8,128)(2,1)} fusion(bf16[1,8,2,128,128]{4,3,2,1,0:T(8,128)(2,1)S(1)} %collective-permute-done.1, bf16[1,8,2,128,128]{4,3,2,1,0:T(8,128)(2,1)S(1)} %bitcast.220, bf16[1,8,2,128,128]{4,3,2,1,0:T(8,128)(2,1)S(1)} %collective-permute-done), kind=kLoop, calls=%fused_computation.10 | loop fusion | flops 1572864 | bytes 3145728 | tf_op jit(solution)/shard_map/concatenate | solution.py:18
  37.3 3.0 %reshape_reshape.2 = bf16[6,131072]{1,0:T(8,128)(2,1)S(1)} reshape(bf16[3,8,2,128,128]{4,3,2,1,0:T(8,128)(2,1)} %pad_maximum_fusion) | data formatting | bytes 3145728 | tf_op jit(solution)/shard_map/reshape;reshape | solution.py:69
  40.3 0.7 fusion.2
  41.0 1.4 %copy.128 = bf16[1,6,1024,128]{3,2,1,0:T(8,128)(2,1)} copy(bf16[1,6,1024,128]{3,1,2,0:T(8,128)(2,1)S(1)} %fusion.2) | data formatting | bytes 3145728
  42.4 4.3 %fusion.56 = bf16[2,4,2,128,128]{3,4,0,2,1:T(8,128)(2,1)} fusion(bf16[3,2,4,2,128,128,1]{5,4,3,2,1,0,6:T(8,128)(2,1)} %bitcast.216, bf16[3,4,2,128,2,128,1]{5,1,3,0,4,2,6:T(4,128)(2,1)} %maximum_bitcast_fusion.1, bf16[3,4,2,128,2,128,1]{3,1,5,0,4,2,6:T(4,128)(2,1)} %maximum_bitcast_fusion), kind=kOutput, calls=%fused_computation.31 | convolution fusion | flops 806354944 | bytes 5242880 | tf_op jit(solution)/shard_map/detcij,dtcjbk->etbik/dot_general | solution.py:75
  46.7 9.2 %collective-permute-start.3 = (bf16[2,4,2,128,128]{3,4,0,2,1:T(8,128)(2,1)}, bf16[2,4,2,128,128]{3,4,0,2,1:T(8,128)(2,1)}, u32[]{:S(2)}, u32[]{:S(2)}) collective-permute-start(bf16[2,4,2,128,128]{3,4,0,2,1:T(8,128)(2,1)} %fusion.56), channel_id=1, source_target_pairs={{15,0},{0,1},{1,2},{2,3},{3,4},{4,5},{5,6},{6,7},{7,8},{8,9},{9,10... | collective-permute-start | bytes 1572872 | tf_op jit(solution)/shard_map/ppermute | solution.py:25
  55.8 0.7 fusion
  56.5 1.4 %copy.126 = bf16[1,6,1024,128]{3,2,1,0:T(8,128)(2,1)} copy(bf16[1,6,1024,128]{3,1,2,0:T(8,128)(2,1)S(1)} %fusion) | data formatting | bytes 3145728
  57.9 4.3 %fusion.51 = bf16[2,4,2,128,128]{3,4,0,2,1:T(8,128)(2,1)} fusion(bf16[3,2,4,2,128,128,1]{5,4,3,2,1,0,6:T(8,128)(2,1)} %bitcast.217, bf16[3,4,2,128,2,128,1]{5,1,3,0,4,2,6:T(4,128)(2,1)} %maximum_bitcast_fusion.1, bf16[3,4,2,128,2,128,1]{3,1,5,0,4,2,6:T(4,128)(2,1)} %maximum_bitcast_fusion), kind=kOutput, calls=%fused_computation.30 | convolution fusion | flops 806354944 | bytes 5242880 | tf_op jit(solution)/shard_map/detcij,dtcjbk->etbik/dot_general | solution.py:75
  62.2 1.9 %collective-permute-start.2 = (bf16[2,4,2,128,128]{3,4,0,2,1:T(8,128)(2,1)}, bf16[2,4,2,128,128]{3,4,0,2,1:T(8,128)(2,1)}, u32[]{:S(2)}, u32[]{:S(2)}) collective-permute-start(bf16[2,4,2,128,128]{3,4,0,2,1:T(8,128)(2,1)} %fusion.51), channel_id=1, source_target_pairs={{1,0},{2,1},{3,2},{4,3},{5,4},{6,5},{7,6},{8,7},{9,8},{10,9},{11,1... | collective-permute-start | bytes 1572872 | tf_op jit(solution)/shard_map/ppermute | solution.py:25
  64.5 0.7 fusion.1
  65.2 0.2 copy.127
  65.4 12.8 %collective-permute-done.3 = bf16[2,4,2,128,128]{3,4,0,2,1:T(8,128)(2,1)} collective-permute-done((bf16[2,4,2,128,128]{3,4,0,2,1:T(8,128)(2,1)}, bf16[2,4,2,128,128]{3,4,0,2,1:T(8,128)(2,1)}, u32[]{:S(2)}, u32[]{:S(2)}) %collective-permute-start.3) | collective-permute-done | bytes 524320 | tf_op jit(solution)/shard_map/ppermute | solution.py:25
  78.1 21.8 %collective-permute-done.2 = bf16[2,4,2,128,128]{3,4,0,2,1:T(8,128)(2,1)} collective-permute-done((bf16[2,4,2,128,128]{3,4,0,2,1:T(8,128)(2,1)}, bf16[2,4,2,128,128]{3,4,0,2,1:T(8,128)(2,1)}, u32[]{:S(2)}, u32[]{:S(2)}) %collective-permute-start.2) | collective-permute-done | bytes 524320 | tf_op jit(solution)/shard_map/ppermute | solution.py:25
  99.9 3.4 %fusion.72 = bf16[1,2,4,2,128,128]{4,5,1,3,2,0:T(8,128)(2,1)S(1)} fusion(bf16[2,4,2,128,128]{3,4,0,2,1:T(8,128)(2,1)} %collective-permute-done.3, bf16[2,4,2,128,128]{3,4,0,2,1:T(8,128)(2,1)} %collective-permute-done.2, bf16[3,2,4,2,128,128,1]{5,4,3,2,1,0,6:T(8,128)(2,1)S(1)} %bitcast.215, bf16[3,4,2,128,2,128,1]{5,1,3,0,4,2,6:T(4,128)(2,1)} %maximum_bitcast_fusion.1, ...), kind=kOutput, calls=%fused_computation.48 | convolution fusion | flops 807403520 | bytes 6291456 | tf_op jit(solution)/shard_map/detcij,dtcjbk->etbik/dot_general | solution.py:75
  103.3 1.0 copy.77
  (26 shorter events, 1.4 us)
Async XLA Ops:
  0.0 7.8 %copy-start = (bf16[3,4,2,128,128]{4,3,2,1,0:T(8,128)(2,1)S(1)}, bf16[3,4,2,128,128]{4,3,2,1,0:T(8,128)(2,1)}, u32[]{:S(2)}) copy-start(bf16[3,4,2,128,128]{4,3,2,1,0:T(8,128)(2,1)} %param.6) | copy-start | bytes 2359300
  0.0 17.6 %collective-permute-start.1 = (bf16[1,8,2,128,128]{4,3,2,1,0:T(8,128)(2,1)}, bf16[1,8,2,128,128]{4,3,2,1,0:T(8,128)(2,1)S(1)}, u32[]{:S(2)}, u32[]{:S(2)}) collective-permute-start(bf16[1,8,2,128,128]{4,3,2,1,0:T(8,128)(2,1)} %bitcast.218), channel_id=1, source_target_pairs={{16,0},{32,16},{48,32},{64,48},{80,64},{96,80},{112,96},{128,112},... | collective-permute-start | bytes 1572872 | tf_op jit(solution)/shard_map/ppermute | solution.py:17
  2.1 33.9 %collective-permute-start = (bf16[1,8,2,128,128]{4,3,2,1,0:T(8,128)(2,1)}, bf16[1,8,2,128,128]{4,3,2,1,0:T(8,128)(2,1)S(1)}, u32[]{:S(2)}, u32[]{:S(2)}) collective-permute-start(bf16[1,8,2,128,128]{4,3,2,1,0:T(8,128)(2,1)} %bitcast.219), channel_id=1, source_target_pairs={{0,16},{16,32},{32,48},{48,64},{64,80},{80,96},{96,112},{112,128},... | collective-permute-start | bytes 1572872 | tf_op jit(solution)/shard_map/ppermute | solution.py:14
  8.5 0.7 copy-start.2
  15.3 20.7 %copy-start.1 = (bf16[1,2,4,2,128,128]{5,4,3,2,1,0:T(8,128)(2,1)S(1)}, bf16[1,2,4,2,128,128]{5,4,3,2,1,0:T(8,128)(2,1)}, u32[]{:S(2)}) copy-start(bf16[1,2,4,2,128,128]{5,4,3,2,1,0:T(8,128)(2,1)} %param.5) | copy-start | bytes 1572868
  46.7 31.5 %collective-permute-start.3 = (bf16[2,4,2,128,128]{3,4,0,2,1:T(8,128)(2,1)}, bf16[2,4,2,128,128]{3,4,0,2,1:T(8,128)(2,1)}, u32[]{:S(2)}, u32[]{:S(2)}) collective-permute-start(bf16[2,4,2,128,128]{3,4,0,2,1:T(8,128)(2,1)} %fusion.56), channel_id=1, source_target_pairs={{15,0},{0,1},{1,2},{2,3},{3,4},{4,5},{5,6},{6,7},{7,8},{8,9},{9,10... | collective-permute-start | bytes 1572872 | tf_op jit(solution)/shard_map/ppermute | solution.py:25
  62.2 37.7 %collective-permute-start.2 = (bf16[2,4,2,128,128]{3,4,0,2,1:T(8,128)(2,1)}, bf16[2,4,2,128,128]{3,4,0,2,1:T(8,128)(2,1)}, u32[]{:S(2)}, u32[]{:S(2)}) collective-permute-start(bf16[2,4,2,128,128]{3,4,0,2,1:T(8,128)(2,1)} %fusion.51), channel_id=1, source_target_pairs={{1,0},{2,1},{3,2},{4,3},{5,4},{6,5},{7,6},{8,7},{9,8},{10,9},{11,1... | collective-permute-start | bytes 1572872 | tf_op jit(solution)/shard_map/ppermute | solution.py:25

commit v2 on v1

v2 whole, which is shorter than its diff:
```python
import functools

import jax
import jax.numpy as jnp
from jax import lax
from jax.experimental import pallas as pl
from jax.experimental.pallas import tpu as pltpu
from jax.sharding import PartitionSpec as P

MESH = pl.DeviceIdType.MESH
F32, BF16 = jnp.float32, jnp.bfloat16
ZLO, YS, CORES, EB, NB, RANGE = 8, 4, 2, 2, 3, 2
SPAN = 2 * RANGE + 1
ROWS = 16


def spot(e, k):
    return {"energy": e, "momentum": k}


def kernel(
    ne, nk, weight, modes, pattern, green, dham, out,
    mine, blocks, coef, left, right, mixed, prod, near, passing, part, gained, own,
    load_sem, m_send, m_recv, r_send, r_recv, e_send, e_recv,
):
    nt, ts = green.shape[1], green.shape[3]
    e, k = lax.axis_index("energy"), lax.axis_index("momentum")
    core, y, z_hi = k % CORES, (k // CORES) % YS, k // (CORES * YS)
    z_lo, x = e % ZLO, e // ZLO

    def at(plane, c, side):
        turn = jnp.where(z_lo < ZLO // 2, side, 1 - side)
        return spot(
            x * ZLO + (z_lo + ZLO // 2) % ZLO, (((z_hi + turn) % 2) * YS + plane) * CORES + c
        )

    up_far = jnp.logical_and(y == YS - 1, core == 1)
    down_far = jnp.logical_and(y == 0, core == 0)
    relays = jnp.logical_or(y == 1, y == 2)
    above, below = (k + 1) % nk, (k + nk - 1) % nk

    loads = [
        pltpu.make_async_copy(green, mine, load_sem.at[0]),
        pltpu.make_async_copy(dham, blocks, load_sem.at[1]),
    ]
    for load in loads:
        load.start()

    barrier = pltpu.get_barrier_semaphore()

    def greet(where):
        pl.semaphore_signal(barrier, inc=1, device_id=where, device_id_type=MESH)

    @pl.when(down_far)
    def _():
        greet(at(2, 0, 1))
        greet(at(2, 1, 0))

    @pl.when(jnp.logical_not(down_far))
    def _():
        greet(spot(e, below))

    @pl.when(up_far)
    def _():
        greet(at(1, 0, 1))
        greet(at(1, 1, 0))

    @pl.when(jnp.logical_not(up_far))
    def _():
        greet(spot(e, above))

    def relay_source():
        return (y == 2), (core == 0)

    for plane, (source_y, source_c) in ((1, (0, 0)), (2, (YS - 1, 1))):
        for c in (0, 1):

            @pl.when(jnp.logical_and(y == plane, core == c))
            def _():
                greet(at(source_y, source_c, 1 - c))

    @pl.when(e > 0)
    def _():
        greet(spot(e - 1, k))

    @pl.when(e < ne - 1)
    def _():
        greet(spot(e + 1, k))

    lane = lax.broadcasted_iota(jnp.int32, (8, 128), 1)
    row = lax.broadcasted_iota(jnp.int32, (8, 128), 0)
    lane_q, lane_s = lane // SPAN - 1, lane % SPAN - RANGE
    table = jnp.zeros((8, 128), F32)
    for m in range(modes.shape[0]):
        emit, absorb = [
            jnp.where(row == 0, weight[m, 0, i], jnp.where(row == 1, weight[m, 1, i], weight[m, 2, i]))
            for i in (0, 1)
        ]
        step = modes[m, 1]
        term = jnp.where(lane_s == -step, emit, 0.0) + jnp.where(lane_s == step, absorb, 0.0)
        table = table + jnp.where(lane_q == modes[m, 0], term, 0.0)
    table = table.astype(BF16).astype(F32)
    for q in range(3):
        for d in range(3):
            for s in range(SPAN):
                at_lane = q * SPAN + s
                coef[(q * 3 + d) * SPAN + s] = jnp.broadcast_to(
                    table[d : d + 1, at_lane : at_lane + 1], (8, 128)
                )

    loads[1].wait()

    def stack(t, _):
        for d in range(3):
            re, im = blocks[d, pattern[t, 0], 0], blocks[d, pattern[t, 0], 1]
            left[t, d, :ts, :ts] = re
            left[t, d, :ts, ts:] = -im
            left[t, d, ts:, :ts] = im
            left[t, d, ts:, ts:] = re
            re = blocks[d, pattern[t, 1], 0].astype(F32).T.astype(BF16)
            im = blocks[d, pattern[t, 1], 1].astype(F32).T.astype(BF16)
            base = 2 * ts * d
            right[t, base : base + ts, :ts] = re
            right[t, base : base + ts, ts:] = -im
            right[t, base + ts : base + 2 * ts, :ts] = im
            right[t, base + ts : base + 2 * ts, ts:] = re
        return 0

    lax.fori_loop(0, nt, stack, 0)

    @pl.when(e == 0)
    def _():
        gained[0] = jnp.zeros(gained.shape[1:], BF16)

    @pl.when(e == ne - 1)
    def _():
        gained[1] = jnp.zeros(gained.shape[1:], BF16)

    far = jnp.logical_or(up_far, down_far)
    pl.semaphore_wait(
        barrier,
        2
        + far.astype(jnp.int32)
        + relays.astype(jnp.int32)
        + (e > 0).astype(jnp.int32)
        + (e < ne - 1).astype(jnp.int32),
    )

    def direct(t, i, way):
        target = above if way == 0 else below
        return pltpu.make_async_remote_copy(
            src_ref=green.at[i, t], dst_ref=near.at[way, t, i],
            send_sem=m_send.at[way, t, i], recv_sem=m_recv.at[way, t, i],
            device_id=spot(e, target), device_id_type=MESH,
        )

    def detour(t, i, way):
        return pltpu.make_async_remote_copy(
            src_ref=green.at[i, t], dst_ref=passing.at[t],
            send_sem=m_send.at[way, t, i], recv_sem=r_recv.at[t],
            device_id=at(2 if way == 0 else 1, i, i), device_id_type=MESH,
        )

    def forward(t, plane, c):
        goal_y, goal_c, way = (0, 0, 0) if plane == 2 else (YS - 1, 1, 1)
        return pltpu.make_async_remote_copy(
            src_ref=passing.at[t], dst_ref=near.at[way, t, c],
            send_sem=r_send.at[t], recv_sem=m_recv.at[way, t, c],
            device_id=at(goal_y, goal_c, c), device_id_type=MESH,
        )

    def send_raw(t, _):
        for way, is_far in ((0, up_far), (1, down_far)):
            for i in range(EB):

                @pl.when(is_far)
                def _():
                    detour(t, i, way).start()

                @pl.when(jnp.logical_not(is_far))
                def _():
                    direct(t, i, way).start()

        return 0

    lax.fori_loop(0, nt, send_raw, 0)
    loads[0].wait()

    outer = [0, 1, 4, 5]
    inner = [2, 3]

    def contract(t, targets):
        width = len(targets) * ts

        def mix(c):
            def rows(j, _):
                at_row = pl.multiple_of(j * ROWS, ROWS)
                tiles = [
                    [
                        ref[c, pl.ds(at_row, ROWS), :].astype(F32).reshape(ROWS // 8, 8, ts)
                        for ref in refs
                    ]
                    for refs in (
                        [near.at[1, t, i] for i in range(EB)],
                        [mine.at[i, t] for i in range(EB)],
                        [near.at[0, t, i] for i in range(EB)],
                    )
                ]
                for d in range(3):
                    for n, target in enumerate(targets):
                        total = None
                        for i in range(EB):
                            s = i - (target - RANGE)
                            if abs(s) > RANGE:
                                continue
                            for q in range(3):
                                value = coef[(q * 3 + d) * SPAN + s + RANGE][None] * tiles[q][i]
                                total = value if total is None else total + value
                        mixed[d, pl.ds(c * ts + at_row, ROWS), n * ts : (n + 1) * ts] = (
                            total.reshape(ROWS, ts).astype(BF16)
                        )
                return 0

            lax.fori_loop(0, ts // ROWS, rows, 0)

        mix(0)
        mix(1)
        for d in range(3):
            got = jnp.dot(left[t, d], mixed[d, :, :width], preferred_element_type=F32).astype(BF16)
            for n in range(len(targets)):
                for c in range(2):
                    prod[n * ts : (n + 1) * ts, (2 * d + c) * ts : (2 * d + c + 1) * ts] = got[
                        c * ts : (c + 1) * ts, n * ts : (n + 1) * ts
                    ]
        return jnp.dot(prod[:width], right[t], preferred_element_type=F32)

    def shift(t, way):
        return pltpu.make_async_remote_copy(
            src_ref=part.at[way, t], dst_ref=gained.at[1 - way, t],
            send_sem=e_send.at[way, t], recv_sem=e_recv.at[1 - way, t],
            device_id=spot(e - 1 if way == 0 else e + 1, k), device_id_type=MESH,
        )

    def tile(t, _):
        for side in (0, 1):
            for i in range(EB):
                direct(t, i, side).wait_recv()
        total = contract(t, outer)
        for n in range(4):
            for c in range(2):
                part[n // 2, t, n % 2, c] = total[
                    n * ts : (n + 1) * ts, c * ts : (c + 1) * ts
                ].astype(BF16)

        @pl.when(e > 0)
        def _():
            shift(t, 0).start()

        @pl.when(e < ne - 1)
        def _():
            shift(t, 1).start()

        for plane in (1, 2):
            for c in (0, 1):

                @pl.when(jnp.logical_and(y == plane, core == c))
                def _():
                    hop = forward(t, plane, c)
                    detour(t, c, 0).wait_recv()
                    hop.start()

        total = contract(t, inner)
        for n in range(2):
            for c in range(2):
                own[t, n, c] = total[n * ts : (n + 1) * ts, c * ts : (c + 1) * ts]
        return 0

    lax.fori_loop(0, nt, tile, 0)

    def finish(t, _):
        @pl.when(e > 0)
        def _():
            shift(t, 1).wait_recv()

        @pl.when(e < ne - 1)
        def _():
            shift(t, 0).wait_recv()

        for n in range(EB):
            out[n, t] = (
                own[t, n] + gained[0, t, n].astype(F32) + gained[1, t, n].astype(F32)
            ).astype(BF16)
        return 0

    lax.fori_loop(0, nt, finish, 0)

    def drain(t, _):
        for way in (0, 1):
            for i in range(EB):
                direct(t, i, way).wait_send()

        @pl.when(e > 0)
        def _():
            shift(t, 0).wait_send()

        @pl.when(e < ne - 1)
        def _():
            shift(t, 1).wait_send()

        @pl.when(relays)
        def _():
            forward(t, 1, 0).wait_send()

        return 0

    lax.fori_loop(0, nt, drain, 0)


def solution(mesh):
    ne, nk = mesh.shape["energy"], mesh.shape["momentum"]

    def local(green_tiles, dham_blocks, phonon_weight, phonon_modes, tile_pattern):
        green = green_tiles[0]
        eb, nt, parts, ts, _ = green.shape
        dirs = dham_blocks.shape[0]
        sems = pltpu.SemaphoreType.DMA
        whole = pl.BlockSpec(memory_space=pltpu.SMEM)
        away = pl.BlockSpec(memory_space=pl.ANY)
        got = pl.pallas_call(
            functools.partial(kernel, ne, nk),
            out_shape=jax.ShapeDtypeStruct(green.shape, BF16),
            in_specs=[whole, whole, whole, away, away],
            out_specs=pl.BlockSpec(memory_space=pltpu.VMEM),
            scratch_shapes=[
                pltpu.VMEM(green.shape, BF16),
                pltpu.VMEM(dham_blocks.shape, BF16),
                pltpu.VMEM((3 * dirs * SPAN, 8, 128), F32),
                pltpu.VMEM((nt, dirs, 2 * ts, 2 * ts), BF16),
                pltpu.VMEM((nt, 2 * ts * dirs, 2 * ts), BF16),
                pltpu.VMEM((dirs, 2 * ts, 4 * ts), BF16),
                pltpu.VMEM((4 * ts, 2 * ts * dirs), BF16),
                pltpu.VMEM((2, nt, eb, parts, ts, ts), BF16),
                pltpu.VMEM((nt, parts, ts, ts), BF16),
                pltpu.VMEM((2, nt, eb, parts, ts, ts), BF16),
                pltpu.VMEM((2, nt, eb, parts, ts, ts), BF16),
                pltpu.VMEM((nt, eb, parts, ts, ts), F32),
                sems((2,)),
                sems((2, nt, eb)),
                sems((2, nt, eb)),
                sems((nt,)),
                sems((nt,)),
                sems((2, nt)),
                sems((2, nt)),
            ],
            compiler_params=pltpu.CompilerParams(collective_id=0, has_side_effects=True),
        )(phonon_weight, phonon_modes, tile_pattern, green, dham_blocks)
        return got[None]

    placed = (P("momentum", "energy", None, None, None, None), P(), P(), P(), P())
    return jax.shard_map(
        local,
        mesh=mesh,
        in_specs=placed,
        out_specs=P("momentum", "energy", None, None, None, None),
        check_vma=False,
    )
```

time: 105 us -> 73 us (0.70)
  the two profiles are of different devices: /device:TPU:63 before, /device:TPU:6 now
where the time goes in v2:
time: 73 us; the launch traced here: 72.3 us
  Pallas kernels  67.7 us (93%)
  local copies, waits for them, and re-layouts  4.63 us (6%)
    pallas_call x1, Pallas kernels, local(): pl.pallas_call(functools.partial(kernel, ne, nk), out_shape=jax.ShapeDtyp...  67.7 us
    unnamed x10, local copies, waits for them, and re-layouts  4.63 us

profile of v2, /device:TPU:6, one launch (start us, length us, event | category | flops | bytes accessed | tf_op | source)
XLA Modules:
  0.0 72.3 jit_solution(517213626591943728)
XLA Ops:
  0.0 0.0 copy-start.1
  0.0 0.7 copy-done.1
  0.7 0.0 copy-start.2
  0.7 0.7 copy.8.pattern
  1.4 0.0 copy-done.2
  1.4 0.0 copy-start
  1.4 0.7 copy.7.modes
  2.0 0.0 copy-done
  2.0 0.7 copy.6.weight
  2.8 67.7 %shard_map.55 = bf16[2,4,2,128,128]{4,3,2,1,0:T(8,128)(2,1)} custom-call(f32[6,3,2]{2,1,0:T(4,128)} %copy.6.weight, s32[6,2]{1,0:T(8,128)} %copy.7.modes, s32[4,2]{1,0:T(4,128)} %copy.8.pattern, bf16[2,4,2,128,128]{4,3,2,1,0:T(8,128)(2,1)} %bitcast.3, bf16[3,4,2,128,128]{4,3,2,1,0:T(8,128)(2,1)} %dham.1), custom_call_target="tpu_custom_call" | custom-call | tf_op jit(solution)/shard_map/pallas_call | solution.py:329
  70.4 1.9 %copy.10 = bf16[1,2,4,2,128,128]{5,4,3,2,1,0:T(8,128)(2,1)} copy(bf16[1,2,4,2,128,128]{5,4,3,2,1,0:T(8,128)(2,1)} %bitcast.2) | data formatting | bytes 1048576
Async XLA Ops:
  0.0 0.7 copy-start.1
  0.7 0.7 copy-start.2
  1.4 0.7 copy-start

commit v3 on v2

v3 whole, which is shorter than its diff:
```python
import functools

import jax
import jax.numpy as jnp
from jax import lax
from jax.experimental import pallas as pl
from jax.experimental.pallas import tpu as pltpu
from jax.sharding import PartitionSpec as P

MESH = pl.DeviceIdType.MESH
F32, BF16 = jnp.float32, jnp.bfloat16
ND, H0, H1, HF0, HF1 = 1, 1, 0, 1, 1
ZLO, YS, CORES, EB, NB, RANGE = 8, 4, 2, 2, 3, 2
SPAN = 2 * RANGE + 1
ROWS = 16


def spot(e, k):
    return {"energy": e, "momentum": k}


def kernel(
    ne, nk, weight, modes, pattern, green, dham, own, from_below, from_above,
    mine, blocks, coef, left, right, mixed, prod, near, passing, part, ready,
    load_sem, m_send, m_recv, r_send, r_recv, e_send, e_recv,
):
    nt, ts = green.shape[1], green.shape[3]
    e, k = lax.axis_index("energy"), lax.axis_index("momentum")
    core, y, z_hi = k % CORES, (k // CORES) % YS, k // (CORES * YS)
    z_lo, x = e % ZLO, e // ZLO

    def at(plane, c, side):
        turn = jnp.where(z_lo < ZLO // 2, side, 1 - side)
        return spot(
            x * ZLO + (z_lo + ZLO // 2) % ZLO, (((z_hi + turn) % 2) * YS + plane) * CORES + c
        )

    up_far = jnp.logical_and(y == YS - 1, core == 1)
    down_far = jnp.logical_and(y == 0, core == 0)
    relays = jnp.logical_or(y == 1, y == 2)
    above, below = (k + 1) % nk, (k + nk - 1) % nk

    loads = [
        pltpu.make_async_copy(green, mine, load_sem.at[0]),
        pltpu.make_async_copy(dham, blocks, load_sem.at[1]),
    ]
    for load in loads:
        load.start()

    barrier = pltpu.get_barrier_semaphore()

    def greet(where):
        pl.semaphore_signal(barrier, inc=1, device_id=where, device_id_type=MESH)

    z = z_hi * ZLO + z_lo
    ahead, behind = (z + ZLO // 2) % (2 * ZLO), (z + 3 * ZLO // 2) % (2 * ZLO)

    def answered(source, target):
        return jnp.logical_and(source < ZLO, target > source)

    def relayed(source, target):
        return jnp.logical_or(target >= ZLO, answered(source, target))

    def also(flag, other):
        return jnp.logical_and(flag, other)

    def no(flag):
        return jnp.logical_not(flag)

    count, answers = jnp.int32(0), []

    def meet(flag, where):
        pl.when(flag)(lambda: greet(where))

    def expect(flag):
        nonlocal count
        count = count + flag.astype(jnp.int32)

    meet(no(down_far), spot(e, below))
    meet(no(up_far), spot(e, above))
    expect(no(down_far))
    expect(no(up_far))
    low_end, high_end = also(z_lo == 0, e > 0), also(z_lo == ZLO - 1, e < ne - 1)
    meet(e > 0, spot(e - 1, k))
    meet(also(e < ne - 1, no(also(high_end, z_hi == 0))), spot(e + 1, k))
    expect(also(e > 0, no(also(low_end, z_hi == 0))))
    expect(e < ne - 1)
    answers.append((also(high_end, z_hi == 0), spot(e + 1, k), 3))
    far_waits, relay_waits = [], jnp.bool_(False)
    for mine_far, out_plane, in_plane in ((up_far, 2, 1), (down_far, 1, 2)):
        for c, (there, back) in enumerate(((ahead, behind), (behind, ahead))):
            late = answered(z, there)
            meet(also(mine_far, late), at(out_plane, c, c))
            expect(also(mine_far, no(late)))
            if mine_far is up_far:
                far_waits.append(late)
            late = relayed(back, z)
            meet(also(mine_far, no(late)), at(in_plane, c, 1 - c))
            expect(also(mine_far, late))
            answers.append((also(mine_far, late), at(in_plane, c, 1 - c), 2))
    for mine_far, end in ((up_far, spot(e, above)), (down_far, spot(e, below))):
        if ND:
            meet(also(mine_far, z_hi == 0), end)
            expect(also(mine_far, z_hi == 1))
            answers.append((also(mine_far, z_hi == 1), end, 4))
    for plane, source, goal in ((1, (0, 0), (YS - 1, 1)), (2, (YS - 1, 1), (0, 0))):
        for c, (there, back) in enumerate(((ahead, behind), (behind, ahead))):
            here = also(y == plane, core == c)
            late = answered(back, z)
            meet(also(here, no(late)), at(*source, 1 - c))
            expect(also(here, late))
            answers.append((also(here, late), at(*source, 1 - c), c))
            late = relayed(z, there)
            meet(also(here, late), at(*goal, c))
            expect(also(here, no(late)))
            relay_waits = jnp.logical_or(relay_waits, also(here, late))

    pl.semaphore_wait(barrier, count)
    for flag, where, slot in answers:

        @pl.when(flag)
        def _():
            pl.semaphore_signal(ready.at[slot], inc=1, device_id=where, device_id_type=MESH)

    far = jnp.logical_or(up_far, down_far)

    def direct(t, i, way):
        target = above if way == 0 else below
        return pltpu.make_async_remote_copy(
            src_ref=green.at[i, t], dst_ref=near.at[way, t, i],
            send_sem=m_send.at[way, t, i], recv_sem=m_recv.at[way, t, i],
            device_id=spot(e, target), device_id_type=MESH,
        )

    def detour(t, i, way):
        return pltpu.make_async_remote_copy(
            src_ref=green.at[i, t], dst_ref=passing.at[t],
            send_sem=m_send.at[way, t, i], recv_sem=r_recv.at[t],
            device_id=at(2 if way == 0 else 1, i, i), device_id_type=MESH,
        )

    def forward(t, plane, c):
        goal_y, goal_c, way = (0, 0, 0) if plane == 2 else (YS - 1, 1, 1)
        return pltpu.make_async_remote_copy(
            src_ref=passing.at[t], dst_ref=near.at[way, t, c],
            send_sem=r_send.at[t], recv_sem=m_recv.at[way, t, c],
            device_id=at(goal_y, goal_c, c), device_id_type=MESH,
        )

    def send_near(t, _):
        for way, is_far in ((0, up_far), (1, down_far)):
            for i in range(EB):

                @pl.when(no(is_far))
                def _():
                    direct(t, i, way).start()

        return 0

    lax.fori_loop(0, nt, send_near, 0)
    for i in range(EB):

        @pl.when(also(far, far_waits[i]))
        def _():
            pl.semaphore_wait(ready.at[i], 1)

    for way, is_far in ((0, up_far), (1, down_far)):

        @pl.when(is_far)
        def _():
            def send_far(t, _):
                for i in range(EB):
                    detour(t, i, way).start()
                return 0

            def send_straight(t, _):
                for i in range(EB):
                    direct(t, i, way).start()
                return 0

            lax.fori_loop(0, nt - ND, send_far, 0)
            if ND:

                @pl.when(z_hi == 0)
                def _():
                    pl.semaphore_wait(ready.at[4], 1)

                lax.fori_loop(nt - ND, nt, send_straight, 0)

    blank = [
        pltpu.make_async_copy(part.at[0], from_below, load_sem.at[2]),
        pltpu.make_async_copy(part.at[0], from_above, load_sem.at[2]),
    ]
    for edge, copy in zip((e == 0, e == ne - 1), blank):

        @pl.when(edge)
        def _():
            part[0] = jnp.zeros(part.shape[1:], BF16)
            copy.start()
            copy.wait()

    lane = lax.broadcasted_iota(jnp.int32, (8, 128), 1)
    row = lax.broadcasted_iota(jnp.int32, (8, 128), 0)
    lane_q, lane_s = lane // SPAN - 1, lane % SPAN - RANGE
    table = jnp.zeros((8, 128), F32)
    for m in range(modes.shape[1]):
        emit, absorb = [
            jnp.where(row == 0, weight[0, i, m], jnp.where(row == 1, weight[1, i, m], weight[2, i, m]))
            for i in (0, 1)
        ]
        step = modes[1, m]
        term = jnp.where(lane_s == -step, emit, 0.0) + jnp.where(lane_s == step, absorb, 0.0)
        table = table + jnp.where(lane_q == modes[0, m], term, 0.0)
    table = table.astype(BF16).astype(F32)
    for q in range(3):
        for d in range(3):
            for s in range(SPAN):
                at_lane = q * SPAN + s
                coef[(q * 3 + d) * SPAN + s] = jnp.broadcast_to(
                    table[d : d + 1, at_lane : at_lane + 1], (8, 128)
                )

    loads[1].wait()

    def stack(t, _):
        for d in range(3):
            re, im = blocks[d, pattern[0, t], 0], blocks[d, pattern[0, t], 1]
            left[t, d, :ts, :ts] = re
            left[t, d, :ts, ts:] = -im
            left[t, d, ts:, :ts] = im
            left[t, d, ts:, ts:] = re
            re = blocks[d, pattern[1, t], 0].astype(F32).T.astype(BF16)
            im = blocks[d, pattern[1, t], 1].astype(F32).T.astype(BF16)
            base = 2 * ts * d
            right[t, base : base + ts, :ts] = re
            right[t, base : base + ts, ts:] = -im
            right[t, base + ts : base + 2 * ts, :ts] = im
            right[t, base + ts : base + 2 * ts, ts:] = re
        return 0

    lax.fori_loop(0, nt, stack, 0)

    loads[0].wait()

    outer = [0, 1, 4, 5]
    inner = [2, 3]

    def contract(t, targets):
        width = len(targets) * ts

        def mix(c):
            def rows(j, _):
                at_row = pl.multiple_of(j * ROWS, ROWS)
                tiles = [
                    [
                        ref[c, pl.ds(at_row, ROWS), :].astype(F32).reshape(ROWS // 8, 8, ts)
                        for ref in refs
                    ]
                    for refs in (
                        [near.at[1, t, i] for i in range(EB)],
                        [mine.at[i, t] for i in range(EB)],
                        [near.at[0, t, i] for i in range(EB)],
                    )
                ]
                for d in range(3):
                    for n, target in enumerate(targets):
                        total = None
                        for i in range(EB):
                            s = i - (target - RANGE)
                            if abs(s) > RANGE:
                                continue
                            for q in range(3):
                                value = coef[(q * 3 + d) * SPAN + s + RANGE][None] * tiles[q][i]
                                total = value if total is None else total + value
                        mixed[d, pl.ds(c * ts + at_row, ROWS), n * ts : (n + 1) * ts] = (
                            total.reshape(ROWS, ts).astype(BF16)
                        )
                return 0

            lax.fori_loop(0, ts // ROWS, rows, 0)

        mix(0)
        mix(1)
        for d in range(3):
            got = jnp.dot(left[t, d], mixed[d, :, :width], preferred_element_type=F32).astype(BF16)
            for n in range(len(targets)):
                for c in range(2):
                    prod[n * ts : (n + 1) * ts, (2 * d + c) * ts : (2 * d + c + 1) * ts] = got[
                        c * ts : (c + 1) * ts, n * ts : (n + 1) * ts
                    ]
        return jnp.dot(prod[:width], right[t], preferred_element_type=F32)

    def shift(t, way):
        return pltpu.make_async_remote_copy(
            src_ref=part.at[way, :, t], dst_ref=(from_above if way == 0 else from_below).at[:, t],
            send_sem=e_send.at[way, t], recv_sem=e_recv.at[1 - way, t],
            device_id=spot(e - 1 if way == 0 else e + 1, k), device_id_type=MESH,
        )

    early = z_hi == 0
    slow = also(low_end, early)

    def hold_near(t):
        return also(relays, t >= jnp.where(early, H0, H1))

    def hold_far(t):
        return also(relays, t >= jnp.where(early, HF0, HF1))

    ways = ((0, e > 0, z_lo == 0), (1, e < ne - 1, z_lo == ZLO - 1))

    def send_parts(t, long, flag):
        for way, there, is_long in ways:

            @pl.when(also(also(there, flag), is_long if long else no(is_long)))
            def _():
                shift(t, way).start()

    def relay(t, _):
        for plane in (1, 2):
            for c in (0, 1):

                @pl.when(also(y == plane, core == c))
                def _():
                    hop = forward(t, plane, c)
                    detour(t, c, 0).wait_recv()

                    @pl.when(also(relay_waits, t == 0))
                    def _():
                        pl.semaphore_wait(ready.at[2], 1)

                    hop.start()

        return 0

    def tile(t, _):
        for side in (0, 1):
            for i in range(EB):
                direct(t, i, side).wait_recv()
        total = contract(t, outer)
        for n in range(4):
            for c in range(2):
                part[n // 2, n % 2, t, c] = total[
                    n * ts : (n + 1) * ts, c * ts : (c + 1) * ts
                ].astype(BF16)

        send_parts(t, True, no(jnp.logical_or(slow, hold_far(t))))
        send_parts(t, False, no(hold_near(t)))

        @pl.when(also(also(relays, no(early)), t < nt - ND))
        def _():
            relay(t, 0)

        total = contract(t, inner)
        for n in range(2):
            for c in range(2):
                own[n, t, c] = total[n * ts : (n + 1) * ts, c * ts : (c + 1) * ts]
        return 0

    lax.fori_loop(0, nt, tile, 0)

    def slow_parts(t, _):
        send_parts(t, True, slow)
        return 0

    @pl.when(slow)
    def _():
        pl.semaphore_wait(ready.at[3], 1)
        lax.fori_loop(0, nt, slow_parts, 0)

    @pl.when(also(relays, early))
    def _():
        lax.fori_loop(0, nt - ND, relay, 0)

    def late(t, _):
        send_parts(t, True, also(hold_far(t), no(slow)))
        send_parts(t, False, hold_near(t))
        return 0

    @pl.when(relays)
    def _():
        lax.fori_loop(0, nt, late, 0)

    def finish(t, _):
        @pl.when(e > 0)
        def _():
            shift(t, 1).wait_recv()

        @pl.when(e < ne - 1)
        def _():
            shift(t, 0).wait_recv()

        return 0

    lax.fori_loop(0, nt, finish, 0)

    def drain(t, _):
        for way in (0, 1):
            for i in range(EB):
                direct(t, i, way).wait_send()

        @pl.when(e > 0)
        def _():
            shift(t, 0).wait_send()

        @pl.when(e < ne - 1)
        def _():
            shift(t, 1).wait_send()

        @pl.when(also(relays, t < nt - ND))
        def _():
            forward(t, 1, 0).wait_send()

        return 0

    lax.fori_loop(0, nt, drain, 0)


def solution(mesh):
    ne, nk = mesh.shape["energy"], mesh.shape["momentum"]

    def local(green_tiles, dham_blocks, phonon_weight, phonon_modes, tile_pattern):
        green = green_tiles[0]
        eb, nt, parts, ts, _ = green.shape
        dirs = dham_blocks.shape[0]
        sems = pltpu.SemaphoreType.DMA
        whole = pl.BlockSpec(memory_space=pltpu.SMEM)
        away = pl.BlockSpec(memory_space=pl.ANY)
        own, from_below, from_above = pl.pallas_call(
            functools.partial(kernel, ne, nk),
            out_shape=[jax.ShapeDtypeStruct(green.shape, kind) for kind in (F32, BF16, BF16)],
            in_specs=[whole, whole, whole, away, away],
            out_specs=[pl.BlockSpec(memory_space=pltpu.VMEM), away, away],
            scratch_shapes=[
                pltpu.VMEM(green.shape, BF16),
                pltpu.VMEM(dham_blocks.shape, BF16),
                pltpu.VMEM((3 * dirs * SPAN, 8, 128), F32),
                pltpu.VMEM((nt, dirs, 2 * ts, 2 * ts), BF16),
                pltpu.VMEM((nt, 2 * ts * dirs, 2 * ts), BF16),
                pltpu.VMEM((dirs, 2 * ts, 4 * ts), BF16),
                pltpu.VMEM((4 * ts, 2 * ts * dirs), BF16),
                pltpu.VMEM((2, nt, eb, parts, ts, ts), BF16),
                pltpu.VMEM((nt, parts, ts, ts), BF16),
                pltpu.VMEM((2, eb, nt, parts, ts, ts), BF16),
                pltpu.SemaphoreType.REGULAR((5,)),
                sems((3,)),
                sems((2, nt, eb)),
                sems((2, nt, eb)),
                sems((nt,)),
                sems((nt,)),
                sems((2, nt)),
                sems((2, nt)),
            ],
            compiler_params=pltpu.CompilerParams(collective_id=0, has_side_effects=True),
        )(phonon_weight.transpose(1, 2, 0), phonon_modes.T, tile_pattern.T, green, dham_blocks)
        return (own + from_below.astype(F32) + from_above.astype(F32)).astype(BF16)[None]

    placed = (P("momentum", "energy", None, None, None, None), P(), P(), P(), P())
    return jax.shard_map(
        local,
        mesh=mesh,
        in_specs=placed,
        out_specs=P("momentum", "energy", None, None, None, None),
        check_vma=False,
    )
```

time: 73 us -> 61.2 us (0.84)
  Pallas kernels: 67.7 us -> 58.5 us
  local copies, waits for them, and re-layouts: 4.63 us -> 0 us
  other arithmetic: 0 us -> 2.51 us
    pallas_call x1, Pallas kernels: 67.7 us -> 58.5 us  [local(): pl.pallas_call(functools.partial(kernel, ne, nk), out_shape=[jax.ShapeDty...]
    unnamed x10 -> x0, local copies, waits for them, and re-layouts: 4.63 us -> none
    broadcast_in_dim x0 -> x1, other arithmetic: none -> 2.51 us  [local(): (own + from_below.astype(F32) + from_above.astype(F32)).astype(BF16)[None]]
where the time goes in v3:
time: 61.2 us; the launch traced here: 61 us
  Pallas kernels  58.5 us (96%)
  other arithmetic  2.51 us (4%)
    pallas_call x1, Pallas kernels, local(): pl.pallas_call(functools.partial(kernel, ne, nk), out_shape=[jax.ShapeDty...  58.5 us
    broadcast_in_dim x1, other arithmetic, local(): (own + from_below.astype(F32) + from_above.astype(F32)).astype(BF16)[None]  2.51 us

profile of v3, /device:TPU:6, one launch (start us, length us, event | category | flops | bytes accessed | tf_op | source)
XLA Modules:
  0.0 61.0 jit_solution(9209235282383593839)
XLA Ops:
  0.0 58.5 %shard_map.55 = (f32[2,4,2,128,128]{4,3,2,1,0:T(8,128)}, bf16[2,4,2,128,128]{4,3,2,1,0:T(8,128)(2,1)}, bf16[2,4,2,128,128]{4,3,2,1,0:T(8,128)(2,1)}) custom-call(f32[3,2,6]{2,1,0:T(2,128)} %bitcast.7, s32[2,6]{1,0:T(2,128)} %bitcast.8, s32[2,4]{1,0:T(2,128)} %bitcast.9, bf16[2,4,2,128,128]{4,3,2,1,0:T(8,128)(2,1)} %bitcast.6, bf16[3,4,2,128,128]{4,3,2,1,0:T(8,128)(2,1)} %dham.1), custom_call_target="tpu_custom_call" | custom-call | tf_op jit(solution)/shard_map/pallas_call | solution.py:428
  58.5 2.5 %fusion = bf16[1,2,4,2,128,128]{5,4,3,2,1,0:T(8,128)(2,1)} fusion(bf16[2,4,2,128,128]{4,3,2,1,0:T(8,128)(2,1)} %get-tuple-element.10, f32[2,4,2,128,128]{4,3,2,1,0:T(8,128)} %get-tuple-element.8, bf16[2,4,2,128,128]{4,3,2,1,0:T(8,128)(2,1)} %get-tuple-element.9), kind=kLoop, calls=%fused_computation.1 | loop fusion | flops 1310720 | bytes 2621440 | tf_op jit(solution)/shard_map/broadcast_in_dim | solution.py:455

commit v4 on v3

--- a/solution.py
+++ b/solution.py
@@ -20,9 +20,9 @@
 
 
 def kernel(
-    ne, nk, weight, modes, pattern, green, dham, own, from_below, from_above,
-    mine, blocks, coef, left, right, mixed, prod, near, passing, part, ready,
-    load_sem, m_send, m_recv, r_send, r_recv, e_send, e_recv,
+    ne, nk, weight, modes, pattern, green, dham, own_out, from_below, from_above,
+    mine, blocks, coef, left, right, mixed, prod, near, passing, part, own, ready,
+    load_sem, own_sem, m_send, m_recv, r_send, r_recv, e_send, e_recv,
 ):
     nt, ts = green.shape[1], green.shape[3]
     e, k = lax.axis_index("energy"), lax.axis_index("momentum")
@@ -76,16 +76,6 @@
         nonlocal count
         count = count + flag.astype(jnp.int32)
 
-    meet(no(down_far), spot(e, below))
-    meet(no(up_far), spot(e, above))
-    expect(no(down_far))
-    expect(no(up_far))
-    low_end, high_end = also(z_lo == 0, e > 0), also(z_lo == ZLO - 1, e < ne - 1)
-    meet(e > 0, spot(e - 1, k))
-    meet(also(e < ne - 1, no(also(high_end, z_hi == 0))), spot(e + 1, k))
-    expect(also(e > 0, no(also(low_end, z_hi == 0))))
-    expect(e < ne - 1)
-    answers.append((also(high_end, z_hi == 0), spot(e + 1, k), 3))
     far_waits, relay_waits = [], jnp.bool_(False)
     for mine_far, out_plane, in_plane in ((up_far, 2, 1), (down_far, 1, 2)):
         for c, (there, back) in enumerate(((ahead, behind), (behind, ahead))):
@@ -115,6 +105,16 @@
             expect(also(here, no(late)))
             relay_waits = jnp.logical_or(relay_waits, also(here, late))
 
+    meet(no(down_far), spot(e, below))
+    meet(no(up_far), spot(e, above))
+    expect(no(down_far))
+    expect(no(up_far))
+    low_end, high_end = also(z_lo == 0, e > 0), also(z_lo == ZLO - 1, e < ne - 1)
+    meet(e > 0, spot(e - 1, k))
+    meet(also(e < ne - 1, no(also(high_end, z_hi == 0))), spot(e + 1, k))
+    expect(also(e > 0, no(also(low_end, z_hi == 0))))
+    expect(e < ne - 1)
+    answers.append((also(high_end, z_hi == 0), spot(e + 1, k), 3))
     pl.semaphore_wait(barrier, count)
     for flag, where, slot in answers:
 
@@ -242,25 +242,20 @@
 
     loads[0].wait()
 
-    outer = [0, 1, 4, 5]
+    outer = [[0, 1], [4, 5]]
     inner = [2, 3]
 
-    def contract(t, targets):
-        width = len(targets) * ts
-
-        def mix(c):
-            def rows(j, _):
-                at_row = pl.multiple_of(j * ROWS, ROWS)
+    def mix(t, targets, slot):
+        sources = (
+            [near.at[1, t, i] for i in range(EB)],
+            [mine.at[i, t] for i in range(EB)],
+            [near.at[0, t, i] for i in range(EB)],
+        )
+        for c in range(2):
+            for j in range(0, ts, ROWS):
                 tiles = [
-                    [
-                        ref[c, pl.ds(at_row, ROWS), :].astype(F32).reshape(ROWS // 8, 8, ts)
-                        for ref in refs
-                    ]
-                    for refs in (
-                        [near.at[1, t, i] for i in range(EB)],
-                        [mine.at[i, t] for i in range(EB)],
-                        [near.at[0, t, i] for i in range(EB)],
-                    )
+                    [ref[c, j : j + ROWS, :].astype(F32).reshape(ROWS // 8, 8, ts) for ref in refs]
+                    for refs in sources
                 ]
                 for d in range(3):
                     for n, target in enumerate(targets):
@@ -272,23 +267,19 @@
                             for q in range(3):
                                 value = coef[(q * 3 + d) * SPAN + s + RANGE][None] * tiles[q][i]
                                 total = value if total is None else total + value
-                        mixed[d, pl.ds(c * ts + at_row, ROWS), n * ts : (n + 1) * ts] = (
+                        mixed[slot, d, c * ts + j : c * ts + j + ROWS, n * ts : (n + 1) * ts] = (
                             total.reshape(ROWS, ts).astype(BF16)
                         )
-                return 0
-
-            lax.fori_loop(0, ts // ROWS, rows, 0)
-
-        mix(0)
-        mix(1)
+
+    def contract(t, slot):
         for d in range(3):
-            got = jnp.dot(left[t, d], mixed[d, :, :width], preferred_element_type=F32).astype(BF16)
-            for n in range(len(targets)):
+            got = jnp.dot(left[t, d], mixed[slot, d], preferred_element_type=F32).astype(BF16)
+            for n in range(EB):
                 for c in range(2):
-                    prod[n * ts : (n + 1) * ts, (2 * d + c) * ts : (2 * d + c + 1) * ts] = got[
+                    prod[slot, n * ts : (n + 1) * ts, (2 * d + c) * ts : (2 * d + c + 1) * ts] = got[
                         c * ts : (c + 1) * ts, n * ts : (n + 1) * ts
                     ]
-        return jnp.dot(prod[:width], right[t], preferred_element_type=F32)
+        return jnp.dot(prod[slot], right[t], preferred_element_type=F32)
 
     def shift(t, way):
         return pltpu.make_async_remote_copy(
@@ -308,12 +299,16 @@
 
     ways = ((0, e > 0, z_lo == 0), (1, e < ne - 1, z_lo == ZLO - 1))
 
+    def send_part(t, way, long, flag):
+        _, there, is_long = ways[way]
+
+        @pl.when(also(also(there, flag), is_long if long else no(is_long)))
+        def _():
+            shift(t, way).start()
+
     def send_parts(t, long, flag):
-        for way, there, is_long in ways:
-
-            @pl.when(also(also(there, flag), is_long if long else no(is_long)))
-            def _():
-                shift(t, way).start()
+        for way in (1, 0):
+            send_part(t, way, long, flag)
 
     def relay(t, _):
         for plane in (1, 2):
@@ -332,28 +327,41 @@
 
         return 0
 
+    def leave(t):
+        return pltpu.make_async_copy(own.at[:, t], own_out.at[:, t], own_sem.at[t])
+
+    def keep(t, _):
+        mix(t, inner, 0)
+        total = contract(t, 0)
+        for n in range(EB):
+            for c in range(2):
+                own[n, t, c] = total[n * ts : (n + 1) * ts, c * ts : (c + 1) * ts]
+        leave(t).start()
+        return 0
+
     def tile(t, _):
         for side in (0, 1):
             for i in range(EB):
                 direct(t, i, side).wait_recv()
-        total = contract(t, outer)
-        for n in range(4):
-            for c in range(2):
-                part[n // 2, n % 2, t, c] = total[
-                    n * ts : (n + 1) * ts, c * ts : (c + 1) * ts
-                ].astype(BF16)
-
-        send_parts(t, True, no(jnp.logical_or(slow, hold_far(t))))
-        send_parts(t, False, no(hold_near(t)))
+        for way in (1, 0):
+            mix(t, outer[way], way)
+            total = contract(t, way)
+            for n in range(EB):
+                for c in range(2):
+                    part[way, n, t, c] = total[
+                        n * ts : (n + 1) * ts, c * ts : (c + 1) * ts
+                    ].astype(BF16)
+            send_part(t, way, True, no(jnp.logical_or(slow, hold_far(t))))
+            send_part(t, way, False, no(hold_near(t)))
 
         @pl.when(also(also(relays, no(early)), t < nt - ND))
         def _():
             relay(t, 0)
 
-        total = contract(t, inner)
-        for n in range(2):
-            for c in range(2):
-                own[n, t, c] = total[n * ts : (n + 1) * ts, c * ts : (c + 1) * ts]
+        @pl.when(far)
+        def _():
+            keep(t, 0)
+
         return 0
 
     lax.fori_loop(0, nt, tile, 0)
@@ -380,6 +388,10 @@
     def _():
         lax.fori_loop(0, nt, late, 0)
 
+    @pl.when(no(far))
+    def _():
+        lax.fori_loop(0, nt, keep, 0)
+
     def finish(t, _):
         @pl.when(e > 0)
         def _():
@@ -394,6 +406,7 @@
     lax.fori_loop(0, nt, finish, 0)
 
     def drain(t, _):
+        leave(t).wait()
         for way in (0, 1):
             for i in range(EB):
                 direct(t, i, way).wait_send()
@@ -429,20 +442,22 @@
             functools.partial(kernel, ne, nk),
             out_shape=[jax.ShapeDtypeStruct(green.shape, kind) for kind in (F32, BF16, BF16)],
             in_specs=[whole, whole, whole, away, away],
-            out_specs=[pl.BlockSpec(memory_space=pltpu.VMEM), away, away],
+            out_specs=[away, away, away],
             scratch_shapes=[
                 pltpu.VMEM(green.shape, BF16),
                 pltpu.VMEM(dham_blocks.shape, BF16),
                 pltpu.VMEM((3 * dirs * SPAN, 8, 128), F32),
                 pltpu.VMEM((nt, dirs, 2 * ts, 2 * ts), BF16),
                 pltpu.VMEM((nt, 2 * ts * dirs, 2 * ts), BF16),
-                pltpu.VMEM((dirs, 2 * ts, 4 * ts), BF16),
-                pltpu.VMEM((4 * ts, 2 * ts * dirs), BF16),
+                pltpu.VMEM((2, dirs, 2 * ts, 2 * ts), BF16),
+                pltpu.VMEM((2, 2 * ts, 2 * ts * dirs), BF16),
                 pltpu.VMEM((2, nt, eb, parts, ts, ts), BF16),
                 pltpu.VMEM((nt, parts, ts, ts), BF16),
                 pltpu.VMEM((2, eb, nt, parts, ts, ts), BF16),
+                pltpu.VMEM(green.shape, F32),
                 pltpu.SemaphoreType.REGULAR((5,)),
                 sems((3,)),
+                sems((nt,)),
                 sems((2, nt, eb)),
                 sems((2, nt, eb)),
                 sems((nt,)),

time: 61.2 us -> 58.7 us (0.959)
  Pallas kernels: 58.5 us -> 55.6 us
    pallas_call x1, Pallas kernels: 58.5 us -> 55.6 us  [local(): pl.pallas_call(functools.partial(kernel, ne, nk), out_shape=[jax.ShapeDty...]
where the time goes in v4:
time: 58.7 us; the launch traced here: 58.1 us
  Pallas kernels  55.6 us (95%)
  other arithmetic  2.51 us (4%)
    pallas_call x1, Pallas kernels, local(): pl.pallas_call(functools.partial(kernel, ne, nk), out_shape=[jax.ShapeDty...  55.6 us
    broadcast_in_dim x1, other arithmetic, local(): (own + from_below.astype(F32) + from_above.astype(F32)).astype(BF16)[None]  2.51 us

profile of v4, /device:TPU:6, one launch (start us, length us, event | category | flops | bytes accessed | tf_op | source)
XLA Modules:
  0.0 58.1 jit_solution(17387519944168772994)
XLA Ops:
  0.0 55.6 %shard_map.55 = (f32[2,4,2,128,128]{4,3,2,1,0:T(8,128)}, bf16[2,4,2,128,128]{4,3,2,1,0:T(8,128)(2,1)}, bf16[2,4,2,128,128]{4,3,2,1,0:T(8,128)(2,1)}) custom-call(f32[3,2,6]{2,1,0:T(2,128)} %bitcast.7, s32[2,6]{1,0:T(2,128)} %bitcast.8, s32[2,4]{1,0:T(2,128)} %bitcast.9, bf16[2,4,2,128,128]{4,3,2,1,0:T(8,128)(2,1)} %bitcast.6, bf16[3,4,2,128,128]{4,3,2,1,0:T(8,128)(2,1)} %dham.1), custom_call_target="tpu_custom_call" | custom-call | tf_op jit(solution)/shard_map/pallas_call | solution.py:441
  55.6 2.5 %fusion = bf16[1,2,4,2,128,128]{5,4,3,2,1,0:T(8,128)(2,1)} fusion(bf16[2,4,2,128,128]{4,3,2,1,0:T(8,128)(2,1)} %get-tuple-element.10, f32[2,4,2,128,128]{4,3,2,1,0:T(8,128)} %get-tuple-element.8, bf16[2,4,2,128,128]{4,3,2,1,0:T(8,128)(2,1)} %get-tuple-element.9), kind=kLoop, calls=%fused_computation.1 | loop fusion | flops 1310720 | bytes 2621440 | tf_op jit(solution)/shard_map/broadcast_in_dim | solution.py:470

commit v5 on v4

--- a/solution.py
+++ b/solution.py
@@ -9,7 +9,7 @@
 
 MESH = pl.DeviceIdType.MESH
 F32, BF16 = jnp.float32, jnp.bfloat16
-ND, H0, H1, HF0, HF1 = 1, 1, 0, 1, 1
+DF, KL, NDE, ND, H0, H1, HF0, HF1 = 0, 1, 1, 1, 1, 0, 1, 1
 ZLO, YS, CORES, EB, NB, RANGE = 8, 4, 2, 2, 3, 2
 SPAN = 2 * RANGE + 1
 ROWS = 16
@@ -20,9 +20,9 @@
 
 
 def kernel(
-    ne, nk, weight, modes, pattern, green, dham, own_out, from_below, from_above,
-    mine, blocks, coef, left, right, mixed, prod, near, passing, part, own, ready,
-    load_sem, own_sem, m_send, m_recv, r_send, r_recv, e_send, e_recv,
+    ne, nk, weight, modes, pattern, green, dham, out,
+    mine, blocks, coef, left, right, mixed, prod, near, passing, part, gained, own, ready,
+    load_sem, m_send, m_recv, r_send, r_recv, e_send, e_recv,
 ):
     nt, ts = green.shape[1], green.shape[3]
     e, k = lax.axis_index("energy"), lax.axis_index("momentum")
@@ -53,6 +53,9 @@
         pl.semaphore_signal(barrier, inc=1, device_id=where, device_id_type=MESH)
 
     z = z_hi * ZLO + z_lo
+    edge = jnp.logical_or(z_lo % (ZLO // 2) == 0, z_lo % (ZLO // 2) == ZLO // 2 - 1)
+    straight = jnp.where(edge, NDE, ND)
+    passed = straight
     ahead, behind = (z + ZLO // 2) % (2 * ZLO), (z + 3 * ZLO // 2) % (2 * ZLO)
 
     def answered(source, target):
@@ -178,26 +181,30 @@
                     direct(t, i, way).start()
                 return 0
 
-            lax.fori_loop(0, nt - ND, send_far, 0)
-            if ND:
-
-                @pl.when(z_hi == 0)
+            if DF:
+
+                @pl.when(z_hi == 1)
                 def _():
-                    pl.semaphore_wait(ready.at[4], 1)
-
-                lax.fori_loop(nt - ND, nt, send_straight, 0)
-
-    blank = [
-        pltpu.make_async_copy(part.at[0], from_below, load_sem.at[2]),
-        pltpu.make_async_copy(part.at[0], from_above, load_sem.at[2]),
-    ]
-    for edge, copy in zip((e == 0, e == ne - 1), blank):
-
-        @pl.when(edge)
-        def _():
-            part[0] = jnp.zeros(part.shape[1:], BF16)
-            copy.start()
-            copy.wait()
+                    lax.fori_loop(nt - straight, nt, send_straight, 0)
+
+            lax.fori_loop(0, nt - straight, send_far, 0)
+
+            @pl.when(z_hi == 0)
+            def _():
+                pl.semaphore_wait(ready.at[4], 1)
+                lax.fori_loop(nt - straight, nt, send_straight, 0)
+
+            if not DF:
+
+                @pl.when(z_hi == 1)
+                def _():
+                    lax.fori_loop(nt - straight, nt, send_straight, 0)
+
+    for side, edge_here in ((0, e == 0), (1, e == ne - 1)):
+
+        @pl.when(edge_here)
+        def _():
+            gained[side] = jnp.zeros(gained.shape[1:], BF16)
 
     lane = lax.broadcasted_iota(jnp.int32, (8, 128), 1)
     row = lax.broadcasted_iota(jnp.int32, (8, 128), 0)
@@ -283,7 +290,7 @@
 
     def shift(t, way):
         return pltpu.make_async_remote_copy(
-            src_ref=part.at[way, :, t], dst_ref=(from_above if way == 0 else from_below).at[:, t],
+            src_ref=part.at[way, :, t], dst_ref=gained.at[1 - way, :, t],
             send_sem=e_send.at[way, t], recv_sem=e_recv.at[1 - way, t],
             device_id=spot(e - 1 if way == 0 else e + 1, k), device_id_type=MESH,
         )
@@ -326,9 +333,6 @@
                     hop.start()
 
         return 0
-
-    def leave(t):
-        return pltpu.make_async_copy(own.at[:, t], own_out.at[:, t], own_sem.at[t])
 
     def keep(t, _):
         mix(t, inner, 0)
@@ -336,7 +340,6 @@
         for n in range(EB):
             for c in range(2):
                 own[n, t, c] = total[n * ts : (n + 1) * ts, c * ts : (c + 1) * ts]
-        leave(t).start()
         return 0
 
     def tile(t, _):
@@ -354,13 +357,15 @@
             send_part(t, way, True, no(jnp.logical_or(slow, hold_far(t))))
             send_part(t, way, False, no(hold_near(t)))
 
-        @pl.when(also(also(relays, no(early)), t < nt - ND))
+        @pl.when(also(also(relays, no(early)), t < nt - passed))
         def _():
             relay(t, 0)
 
-        @pl.when(far)
-        def _():
-            keep(t, 0)
+        if not KL:
+
+            @pl.when(far)
+            def _():
+                keep(t, 0)
 
         return 0
 
@@ -377,7 +382,7 @@
 
     @pl.when(also(relays, early))
     def _():
-        lax.fori_loop(0, nt - ND, relay, 0)
+        lax.fori_loop(0, nt - passed, relay, 0)
 
     def late(t, _):
         send_parts(t, True, also(hold_far(t), no(slow)))
@@ -388,9 +393,13 @@
     def _():
         lax.fori_loop(0, nt, late, 0)
 
-    @pl.when(no(far))
-    def _():
+    if KL:
         lax.fori_loop(0, nt, keep, 0)
+    else:
+
+        @pl.when(no(far))
+        def _():
+            lax.fori_loop(0, nt, keep, 0)
 
     def finish(t, _):
         @pl.when(e > 0)
@@ -401,12 +410,15 @@
         def _():
             shift(t, 0).wait_recv()
 
+        for n in range(EB):
+            out[n, t] = (
+                own[n, t] + gained[0, n, t].astype(F32) + gained[1, n, t].astype(F32)
+            ).astype(BF16)
         return 0
 
     lax.fori_loop(0, nt, finish, 0)
 
     def drain(t, _):
-        leave(t).wait()
         for way in (0, 1):
             for i in range(EB):
                 direct(t, i, way).wait_send()
@@ -419,7 +431,7 @@
         def _():
             shift(t, 1).wait_send()
 
-        @pl.when(also(relays, t < nt - ND))
+        @pl.when(also(relays, t < nt - passed))
         def _():
             forward(t, 1, 0).wait_send()
 
@@ -438,11 +450,11 @@
         sems = pltpu.SemaphoreType.DMA
         whole = pl.BlockSpec(memory_space=pltpu.SMEM)
         away = pl.BlockSpec(memory_space=pl.ANY)
-        own, from_below, from_above = pl.pallas_call(
+        summed = pl.pallas_call(
             functools.partial(kernel, ne, nk),
-            out_shape=[jax.ShapeDtypeStruct(green.shape, kind) for kind in (F32, BF16, BF16)],
+            out_shape=pltpu.VMEM(green.shape, BF16),
             in_specs=[whole, whole, whole, away, away],
-            out_specs=[away, away, away],
+            out_specs=pl.BlockSpec(memory_space=pltpu.VMEM),
             scratch_shapes=[
                 pltpu.VMEM(green.shape, BF16),
                 pltpu.VMEM(dham_blocks.shape, BF16),
@@ -454,10 +466,10 @@
                 pltpu.VMEM((2, nt, eb, parts, ts, ts), BF16),
                 pltpu.VMEM((nt, parts, ts, ts), BF16),
                 pltpu.VMEM((2, eb, nt, parts, ts, ts), BF16),
+                pltpu.VMEM((2, *green.shape), BF16),
                 pltpu.VMEM(green.shape, F32),
                 pltpu.SemaphoreType.REGULAR((5,)),
-                sems((3,)),
-                sems((nt,)),
+                sems((2,)),
                 sems((2, nt, eb)),
                 sems((2, nt, eb)),
                 sems((nt,)),
@@ -467,7 +479,7 @@
             ],
             compiler_params=pltpu.CompilerParams(collective_id=0, has_side_effects=True),
         )(phonon_weight.transpose(1, 2, 0), phonon_modes.T, tile_pattern.T, green, dham_blocks)
-        return (own + from_below.astype(F32) + from_above.astype(F32)).astype(BF16)[None]
+        return summed[None]
 
     placed = (P("momentum", "energy", None, None, None, None), P(), P(), P(), P())
     return jax.shard_map(

time: 58.7 us -> 56.8 us (0.968)
  other arithmetic: 2.51 us -> 0 us
  local copies, waits for them, and re-layouts: 0 us -> 0.8 us
    broadcast_in_dim x1 -> x0, other arithmetic: 2.51 us -> none  [local(): (own + from_below.astype(F32) + from_above.astype(F32)).astype(BF16)[None]]
    unnamed x0 -> x1, local copies, waits for them, and re-layouts: none -> 0.8 us
where the time goes in v5:
time: 56.8 us; the launch traced here: 56.3 us
  Pallas kernels  55.5 us (98%)
  local copies, waits for them, and re-layouts  0.8 us (1%)
    pallas_call x1, Pallas kernels, local(): pl.pallas_call(functools.partial(kernel, ne, nk), out_shape=pltpu.VMEM(gr...  55.5 us

profile of v5, /device:TPU:6, one launch (start us, length us, event | category | flops | bytes accessed | tf_op | source)
XLA Modules:
  0.0 56.3 jit_solution(4312401972546201774)
XLA Ops:
  0.0 55.5 %shard_map.55 = bf16[2,4,2,128,128]{4,3,2,1,0:T(8,128)(2,1)S(1)} custom-call(f32[3,2,6]{2,1,0:T(2,128)} %bitcast.7, s32[2,6]{1,0:T(2,128)} %bitcast.8, s32[2,4]{1,0:T(2,128)} %bitcast.9, bf16[2,4,2,128,128]{4,3,2,1,0:T(8,128)(2,1)} %bitcast.6, bf16[3,4,2,128,128]{4,3,2,1,0:T(8,128)(2,1)} %dham.1), custom_call_target="tpu_custom_call" | custom-call | tf_op jit(solution)/shard_map/pallas_call | solution.py:453
  55.5 0.8 %copy.7 = bf16[1,2,4,2,128,128]{5,4,3,2,1,0:T(8,128)(2,1)} copy(bf16[1,2,4,2,128,128]{5,4,3,2,1,0:T(8,128)(2,1)S(1)} %bitcast.5) | data formatting | bytes 1048576

commit v6 on v5

--- a/solution.py
+++ b/solution.py
@@ -160,7 +160,10 @@
 
         return 0
 
-    lax.fori_loop(0, nt, send_near, 0)
+    @pl.when(no(also(far, z_hi == 1)))
+    def _():
+        lax.fori_loop(0, nt, send_near, 0)
+
     for i in range(EB):
 
         @pl.when(also(far, far_waits[i]))
@@ -199,6 +202,10 @@
                 @pl.when(z_hi == 1)
                 def _():
                     lax.fori_loop(nt - straight, nt, send_straight, 0)
+
+    @pl.when(also(far, z_hi == 1))
+    def _():
+        lax.fori_loop(0, nt, send_near, 0)
 
     for side, edge_here in ((0, e == 0), (1, e == ne - 1)):
 

time: 56.8 us -> 56.8 us (level)
  no operation moved by 1% of the time
where the time goes in v6:
time: 56.8 us; the launch traced here: 56.3 us
  Pallas kernels  55.5 us (98%)
  local copies, waits for them, and re-layouts  0.8 us (1%)
    pallas_call x1, Pallas kernels, local(): pl.pallas_call(functools.partial(kernel, ne, nk), out_shape=pltpu.VMEM(gr...  55.5 us

profile of v6, /device:TPU:6, one launch (start us, length us, event | category | flops | bytes accessed | tf_op | source)
XLA Modules:
  0.0 56.3 jit_solution(12116623617338551889)
XLA Ops:
  0.0 55.5 %shard_map.55 = bf16[2,4,2,128,128]{4,3,2,1,0:T(8,128)(2,1)S(1)} custom-call(f32[3,2,6]{2,1,0:T(2,128)} %bitcast.7, s32[2,6]{1,0:T(2,128)} %bitcast.8, s32[2,4]{1,0:T(2,128)} %bitcast.9, bf16[2,4,2,128,128]{4,3,2,1,0:T(8,128)(2,1)} %bitcast.6, bf16[3,4,2,128,128]{4,3,2,1,0:T(8,128)(2,1)} %dham.1), custom_call_target="tpu_custom_call" | custom-call | tf_op jit(solution)/shard_map/pallas_call | solution.py:460
  55.5 0.8 %copy.7 = bf16[1,2,4,2,128,128]{5,4,3,2,1,0:T(8,128)(2,1)} copy(bf16[1,2,4,2,128,128]{5,4,3,2,1,0:T(8,128)(2,1)S(1)} %bitcast.5) | data formatting | bytes 1048576
